TPU v7x, 512 devices: a whole 4x4x16 slice. The times are simulated.
512 devices in a mesh: row: 8 (over x, y_hi), col: 64 (over y_lo, z, core).
Axes of the slice: x: 4, y: 4 (y_hi: 2, y_lo: 2; y = y_hi * 2 + y_lo), z: 16, core: 2. Of those that a mesh axis runs over, the one named last changes fastest.
Arguments:
- trace_maps: bfloat16 [8, 64, 1280, 1280], P('row', 'col'), may hold values from -0.125 to 0.125
- sources: bfloat16 [8, 64, 1280, 256], P('row', 'col'), may hold values from -6 to 6
Outputs:
- traces: bfloat16 [8, 64, 1280, 256], P('row', 'col')
All inputs are finite; a program needn't handle non-finite values.
Results may differ from a plain program's by a relative error of at most 0.007.
Values may be sent and summed in bfloat16 or wider, within the bound.
A program may use at most 64 MiB of HBM per device.

v0:
```python
import jax
import jax.numpy as jnp
from jax import lax
from jax.sharding import PartitionSpec as P

ITERS = 8


def shifted(array, axis, by):
    count = lax.axis_size(axis)
    pairs = [(i, i + by) for i in range(count) if 0 <= i + by < count]
    return lax.ppermute(array, axis, pairs)


def receive_whole(sent, half):
    left_in = shifted(sent[:half], "col", 1)
    below_in = shifted(sent[half:], "row", 1)
    return jnp.concatenate([left_in, below_in], axis=0)


def update(mapping, incoming, source_float):
    return jnp.dot(mapping, incoming, preferred_element_type=jnp.float32) + source_float


def per_device(trace_maps, sources):
    mapping = trace_maps[0, 0]
    source_float = sources[0, 0].astype(jnp.float32)
    half = mapping.shape[0] // 2
    state = source_float
    for step in range(ITERS):
        incoming = receive_whole(state.astype(jnp.bfloat16), half)
        state = update(mapping, incoming, source_float)
    return state.astype(jnp.bfloat16)[None, None]


def solution(mesh):
    placed = (P("row", "col", None, None), P("row", "col", None, None))
    return jax.shard_map(
        per_device,
        mesh=mesh,
        in_specs=placed,
        out_specs=P("row", "col", None, None),
        check_vma=False,
    )
```

profile of v0, /device:TPU:271, one launch (start us, length us, event | category | flops | bytes accessed | tf_op | source)
XLA Modules:
  0.0 150.5 jit_solution(4347992307303805837)
XLA Ops:
  0.0 2.1 %slice_bitcast_fusion.1 = (bf16[640,256]{1,0:T(8,128)(2,1)}, bf16[640,256]{1,0:T(8,128)(2,1)}) fusion(bf16[1,1,1280,256]{3,2,1,0:T(8,128)(2,1)} %param.3), kind=kLoop, calls=%fused_computation.66 | loop fusion | bytes 1310720 | tf_op jit(solution)/shard_map/slice | solution.py:16
  2.1 3.2 %collective-permute-start = (bf16[640,256]{1,0:T(8,128)(2,1)}, bf16[640,256]{1,0:T(8,128)(2,1)}, u32[]{:S(2)}, u32[]{:S(2)}) collective-permute-start(bf16[640,256]{1,0:T(8,128)(2,1)} %get-tuple-element.19), channel_id=1, source_target_pairs={{0,1},{1,2},{2,3},{3,4},{4,5},{5,6},{6,7},{7,8},{8,9},{9,10},{10,1... | collective-permute-start | bytes 983048 | tf_op jit(solution)/shard_map/ppermute | solution.py:12
  5.3 3.9 %collective-permute-start.1 = (bf16[640,256]{1,0:T(8,128)(2,1)}, bf16[640,256]{1,0:T(8,128)(2,1)}, u32[]{:S(2)}, u32[]{:S(2)}) collective-permute-start(bf16[640,256]{1,0:T(8,128)(2,1)} %get-tuple-element.20), channel_id=1, source_target_pairs={{0,64},{64,128},{128,192},{192,256},{256,320},{320,384},{384,448},... | collective-permute-start | bytes 983048 | tf_op jit(solution)/shard_map/ppermute | solution.py:12
  9.3 2.2 %copy.3 = bf16[1,1,1280,256]{2,3,1,0:T(8,128)(2,1)} copy(bf16[1,1,1280,256]{3,2,1,0:T(8,128)(2,1)} %param.3) | data formatting | bytes 1310720 | tf_op args[1]
  11.4 7.9 %collective-permute-done.1 = bf16[640,256]{1,0:T(8,128)(2,1)} collective-permute-done((bf16[640,256]{1,0:T(8,128)(2,1)}, bf16[640,256]{1,0:T(8,128)(2,1)}, u32[]{:S(2)}, u32[]{:S(2)}) %collective-permute-start.1) | collective-permute-done | bytes 327712 | tf_op jit(solution)/shard_map/ppermute | solution.py:12
  19.4 2.4 %fusion.56 = bf16[1280,256]{0,1:T(8,128)(2,1)S(1)} fusion(bf16[1,1,1280,1280]{3,2,1,0:T(8,128)(2,1)S(1)} %copy-done, bf16[640,256]{1,0:T(8,128)(2,1)} %collective-permute-done.1, bf16[640,256]{1,0:T(8,128)(2,1)} %collective-permute-done, bf16[1,1,1280,256]{2,3,1,0:T(8,128)(2,1)} %copy.3), kind=kOutput, calls=%fused_computation.32 | convolution fusion | flops 841154560 | bytes 5242880 | tf_op jit(solution)/shard_map/dot_general | solution.py:22
  21.8 3.1 %collective-permute-start.2 = (bf16[640,256]{0,1:T(8,128)(2,1)S(1)}, bf16[640,256]{0,1:T(8,128)(2,1)S(1)}, u32[]{:S(2)}, u32[]{:S(2)}) collective-permute-start(bf16[640,256]{0,1:T(8,128)(2,1)S(1)} %get-tuple-element.17), channel_id=1, source_target_pairs={{0,1},{1,2},{2,3},{3,4},{4,5},{5,6},{6,7},{7,8},{8,9},{9,10},{10,1... | collective-permute-start | bytes 983048 | tf_op jit(solution)/shard_map/ppermute | solution.py:12
  24.9 3.0 %collective-permute-start.3 = (bf16[640,256]{0,1:T(8,128)(2,1)S(1)}, bf16[640,256]{0,1:T(8,128)(2,1)S(1)}, u32[]{:S(2)}, u32[]{:S(2)}) collective-permute-start(bf16[640,256]{0,1:T(8,128)(2,1)S(1)} %get-tuple-element.18), channel_id=1, source_target_pairs={{0,64},{64,128},{128,192},{192,256},{256,320},{320,384},{384,448},... | collective-permute-start | bytes 983048 | tf_op jit(solution)/shard_map/ppermute | solution.py:12
  28.9 9.9 %collective-permute-done.3 = bf16[640,256]{0,1:T(8,128)(2,1)S(1)} collective-permute-done((bf16[640,256]{0,1:T(8,128)(2,1)S(1)}, bf16[640,256]{0,1:T(8,128)(2,1)S(1)}, u32[]{:S(2)}, u32[]{:S(2)}) %collective-permute-start.3) | collective-permute-done | bytes 327712 | tf_op jit(solution)/shard_map/ppermute | solution.py:12
  40.0 2.9 %collective-permute-start.4 = (bf16[640,256]{0,1:T(8,128)(2,1)S(1)}, bf16[640,256]{0,1:T(8,128)(2,1)S(1)}, u32[]{:S(2)}, u32[]{:S(2)}) collective-permute-start(bf16[640,256]{0,1:T(8,128)(2,1)S(1)} %get-tuple-element.15), channel_id=1, source_target_pairs={{0,1},{1,2},{2,3},{3,4},{4,5},{5,6},{6,7},{7,8},{8,9},{9,10},{10,1... | collective-permute-start | bytes 983048 | tf_op jit(solution)/shard_map/ppermute | solution.py:12
  42.9 2.1 %collective-permute-start.5 = (bf16[640,256]{0,1:T(8,128)(2,1)S(1)}, bf16[640,256]{0,1:T(8,128)(2,1)S(1)}, u32[]{:S(2)}, u32[]{:S(2)}) collective-permute-start(bf16[640,256]{0,1:T(8,128)(2,1)S(1)} %get-tuple-element.16), channel_id=1, source_target_pairs={{0,64},{64,128},{128,192},{192,256},{256,320},{320,384},{384,448},... | collective-permute-start | bytes 983048 | tf_op jit(solution)/shard_map/ppermute | solution.py:12
  46.9 9.9 %collective-permute-done.5 = bf16[640,256]{0,1:T(8,128)(2,1)S(1)} collective-permute-done((bf16[640,256]{0,1:T(8,128)(2,1)S(1)}, bf16[640,256]{0,1:T(8,128)(2,1)S(1)}, u32[]{:S(2)}, u32[]{:S(2)}) %collective-permute-start.5) | collective-permute-done | bytes 327712 | tf_op jit(solution)/shard_map/ppermute | solution.py:12
  58.0 2.9 %collective-permute-start.6 = (bf16[640,256]{0,1:T(8,128)(2,1)S(1)}, bf16[640,256]{0,1:T(8,128)(2,1)S(1)}, u32[]{:S(2)}, u32[]{:S(2)}) collective-permute-start(bf16[640,256]{0,1:T(8,128)(2,1)S(1)} %get-tuple-element.13), channel_id=1, source_target_pairs={{0,1},{1,2},{2,3},{3,4},{4,5},{5,6},{6,7},{7,8},{8,9},{9,10},{10,1... | collective-permute-start | bytes 983048 | tf_op jit(solution)/shard_map/ppermute | solution.py:12
  60.9 1.9 %collective-permute-start.7 = (bf16[640,256]{0,1:T(8,128)(2,1)S(1)}, bf16[640,256]{0,1:T(8,128)(2,1)S(1)}, u32[]{:S(2)}, u32[]{:S(2)}) collective-permute-start(bf16[640,256]{0,1:T(8,128)(2,1)S(1)} %get-tuple-element.14), channel_id=1, source_target_pairs={{0,64},{64,128},{128,192},{192,256},{256,320},{320,384},{384,448},... | collective-permute-start | bytes 983048 | tf_op jit(solution)/shard_map/ppermute | solution.py:12
  62.8 2.1 %collective-permute-done.6 = bf16[640,256]{0,1:T(8,128)(2,1)S(1)} collective-permute-done((bf16[640,256]{0,1:T(8,128)(2,1)S(1)}, bf16[640,256]{0,1:T(8,128)(2,1)S(1)}, u32[]{:S(2)}, u32[]{:S(2)}) %collective-permute-start.6) | collective-permute-done | bytes 327712 | tf_op jit(solution)/shard_map/ppermute | solution.py:12
  64.9 9.9 %collective-permute-done.7 = bf16[640,256]{0,1:T(8,128)(2,1)S(1)} collective-permute-done((bf16[640,256]{0,1:T(8,128)(2,1)S(1)}, bf16[640,256]{0,1:T(8,128)(2,1)S(1)}, u32[]{:S(2)}, u32[]{:S(2)}) %collective-permute-start.7) | collective-permute-done | bytes 327712 | tf_op jit(solution)/shard_map/ppermute | solution.py:12
  76.0 2.9 %collective-permute-start.8 = (bf16[640,256]{0,1:T(8,128)(2,1)S(1)}, bf16[640,256]{0,1:T(8,128)(2,1)S(1)}, u32[]{:S(2)}, u32[]{:S(2)}) collective-permute-start(bf16[640,256]{0,1:T(8,128)(2,1)S(1)} %get-tuple-element.11), channel_id=1, source_target_pairs={{0,1},{1,2},{2,3},{3,4},{4,5},{5,6},{6,7},{7,8},{8,9},{9,10},{10,1... | collective-permute-start | bytes 983048 | tf_op jit(solution)/shard_map/ppermute | solution.py:12
  78.9 1.9 %collective-permute-start.9 = (bf16[640,256]{0,1:T(8,128)(2,1)S(1)}, bf16[640,256]{0,1:T(8,128)(2,1)S(1)}, u32[]{:S(2)}, u32[]{:S(2)}) collective-permute-start(bf16[640,256]{0,1:T(8,128)(2,1)S(1)} %get-tuple-element.12), channel_id=1, source_target_pairs={{0,64},{64,128},{128,192},{192,256},{256,320},{320,384},{384,448},... | collective-permute-start | bytes 983048 | tf_op jit(solution)/shard_map/ppermute | solution.py:12
  80.8 2.1 %collective-permute-done.8 = bf16[640,256]{0,1:T(8,128)(2,1)S(1)} collective-permute-done((bf16[640,256]{0,1:T(8,128)(2,1)S(1)}, bf16[640,256]{0,1:T(8,128)(2,1)S(1)}, u32[]{:S(2)}, u32[]{:S(2)}) %collective-permute-start.8) | collective-permute-done | bytes 327712 | tf_op jit(solution)/shard_map/ppermute | solution.py:12
  82.9 9.9 %collective-permute-done.9 = bf16[640,256]{0,1:T(8,128)(2,1)S(1)} collective-permute-done((bf16[640,256]{0,1:T(8,128)(2,1)S(1)}, bf16[640,256]{0,1:T(8,128)(2,1)S(1)}, u32[]{:S(2)}, u32[]{:S(2)}) %collective-permute-start.9) | collective-permute-done | bytes 327712 | tf_op jit(solution)/shard_map/ppermute | solution.py:12
  94.0 2.9 %collective-permute-start.10 = (bf16[640,256]{0,1:T(8,128)(2,1)S(1)}, bf16[640,256]{0,1:T(8,128)(2,1)S(1)}, u32[]{:S(2)}, u32[]{:S(2)}) collective-permute-start(bf16[640,256]{0,1:T(8,128)(2,1)S(1)} %get-tuple-element.9), channel_id=1, source_target_pairs={{0,1},{1,2},{2,3},{3,4},{4,5},{5,6},{6,7},{7,8},{8,9},{9,10},{10,1... | collective-permute-start | bytes 983048 | tf_op jit(solution)/shard_map/ppermute | solution.py:12
  96.9 1.9 %collective-permute-start.11 = (bf16[640,256]{0,1:T(8,128)(2,1)S(1)}, bf16[640,256]{0,1:T(8,128)(2,1)S(1)}, u32[]{:S(2)}, u32[]{:S(2)}) collective-permute-start(bf16[640,256]{0,1:T(8,128)(2,1)S(1)} %get-tuple-element.10), channel_id=1, source_target_pairs={{0,64},{64,128},{128,192},{192,256},{256,320},{320,384},{384,448},... | collective-permute-start | bytes 983048 | tf_op jit(solution)/shard_map/ppermute | solution.py:12
  98.8 2.1 %collective-permute-done.10 = bf16[640,256]{0,1:T(8,128)(2,1)S(1)} collective-permute-done((bf16[640,256]{0,1:T(8,128)(2,1)S(1)}, bf16[640,256]{0,1:T(8,128)(2,1)S(1)}, u32[]{:S(2)}, u32[]{:S(2)}) %collective-permute-start.10) | collective-permute-done | bytes 327712 | tf_op jit(solution)/shard_map/ppermute | solution.py:12
  100.9 10.0 %collective-permute-done.11 = bf16[640,256]{0,1:T(8,128)(2,1)S(1)} collective-permute-done((bf16[640,256]{0,1:T(8,128)(2,1)S(1)}, bf16[640,256]{0,1:T(8,128)(2,1)S(1)}, u32[]{:S(2)}, u32[]{:S(2)}) %collective-permute-start.11) | collective-permute-done | bytes 327712 | tf_op jit(solution)/shard_map/ppermute | solution.py:12
  112.0 2.7 %collective-permute-start.12 = (bf16[640,256]{0,1:T(8,128)(2,1)S(1)}, bf16[640,256]{0,1:T(8,128)(2,1)S(1)}, u32[]{:S(2)}, u32[]{:S(2)}) collective-permute-start(bf16[640,256]{0,1:T(8,128)(2,1)S(1)} %get-tuple-element.7), channel_id=1, source_target_pairs={{0,1},{1,2},{2,3},{3,4},{4,5},{5,6},{6,7},{7,8},{8,9},{9,10},{10,1... | collective-permute-start | bytes 983048 | tf_op jit(solution)/shard_map/ppermute | solution.py:12
  116.7 2.1 %collective-permute-done.12 = bf16[640,256]{0,1:T(8,128)(2,1)S(1)} collective-permute-done((bf16[640,256]{0,1:T(8,128)(2,1)S(1)}, bf16[640,256]{0,1:T(8,128)(2,1)S(1)}, u32[]{:S(2)}, u32[]{:S(2)}) %collective-permute-start.12) | collective-permute-done | bytes 327712 | tf_op jit(solution)/shard_map/ppermute | solution.py:12
  118.8 9.9 %collective-permute-done.13 = bf16[640,256]{0,1:T(8,128)(2,1)S(1)} collective-permute-done((bf16[640,256]{0,1:T(8,128)(2,1)S(1)}, bf16[640,256]{0,1:T(8,128)(2,1)S(1)}, u32[]{:S(2)}, u32[]{:S(2)}) %collective-permute-start.13) | collective-permute-done | bytes 327712 | tf_op jit(solution)/shard_map/ppermute | solution.py:12
  129.8 2.8 %collective-permute-start.14 = (bf16[640,256]{0,1:T(8,128)(2,1)S(1)}, bf16[640,256]{0,1:T(8,128)(2,1)S(1)}, u32[]{:S(2)}, u32[]{:S(2)}) collective-permute-start(bf16[640,256]{0,1:T(8,128)(2,1)S(1)} %get-tuple-element.5), channel_id=1, source_target_pairs={{0,1},{1,2},{2,3},{3,4},{4,5},{5,6},{6,7},{7,8},{8,9},{9,10},{10,1... | collective-permute-start | bytes 983048 | tf_op jit(solution)/shard_map/ppermute | solution.py:12
  134.5 2.1 %collective-permute-done.14 = bf16[640,256]{0,1:T(8,128)(2,1)S(1)} collective-permute-done((bf16[640,256]{0,1:T(8,128)(2,1)S(1)}, bf16[640,256]{0,1:T(8,128)(2,1)S(1)}, u32[]{:S(2)}, u32[]{:S(2)}) %collective-permute-start.14) | collective-permute-done | bytes 327712 | tf_op jit(solution)/shard_map/ppermute | solution.py:12
  136.6 9.9 %collective-permute-done.15 = bf16[640,256]{0,1:T(8,128)(2,1)S(1)} collective-permute-done((bf16[640,256]{0,1:T(8,128)(2,1)S(1)}, bf16[640,256]{0,1:T(8,128)(2,1)S(1)}, u32[]{:S(2)}, u32[]{:S(2)}) %collective-permute-start.15) | collective-permute-done | bytes 327712 | tf_op jit(solution)/shard_map/ppermute | solution.py:12
  146.4 1.9 %fusion.80 = bf16[1,1,1280,256]{2,3,1,0:T(8,128)(2,1)} fusion(bf16[1,1,1280,1280]{3,2,1,0:T(8,128)(2,1)S(1)} %copy-done, bf16[640,256]{0,1:T(8,128)(2,1)S(1)} %collective-permute-done.15, bf16[640,256]{0,1:T(8,128)(2,1)S(1)} %collective-permute-done.14, bf16[1,1,1280,256]{2,3,1,0:T(8,128)(2,1)S(1)} %copy-done.1), kind=kOutput, calls=%fused_computation.40 | convolution fusion | flops 841154560 | bytes 5242880 | tf_op jit(solution)/shard_map/dot_general | solution.py:22
  148.4 2.2 %copy.4 = bf16[1,1,1280,256]{3,2,1,0:T(8,128)(2,1)} copy(bf16[1,1,1280,256]{2,3,1,0:T(8,128)(2,1)} %fusion.80) | data formatting | bytes 1310720 | tf_op jit(solution)/shard_map/broadcast_in_dim | solution.py:33
  (22 shorter events, 13.6 us)
Async XLA Ops:
  0.0 19.4 %copy-start = (bf16[1,1,1280,1280]{3,2,1,0:T(8,128)(2,1)S(1)}, bf16[1,1,1280,1280]{3,2,1,0:T(8,128)(2,1)}, u32[]{:S(2)}) copy-start(bf16[1,1,1280,1280]{3,2,1,0:T(8,128)(2,1)} %param.2) | copy-start | bytes 9830404
  2.1 9.3 %collective-permute-start = (bf16[640,256]{1,0:T(8,128)(2,1)}, bf16[640,256]{1,0:T(8,128)(2,1)}, u32[]{:S(2)}, u32[]{:S(2)}) collective-permute-start(bf16[640,256]{1,0:T(8,128)(2,1)} %get-tuple-element.19), channel_id=1, source_target_pairs={{0,1},{1,2},{2,3},{3,4},{4,5},{5,6},{6,7},{7,8},{8,9},{9,10},{10,1... | collective-permute-start | bytes 983048 | tf_op jit(solution)/shard_map/ppermute | solution.py:12
  5.3 14.0 %collective-permute-start.1 = (bf16[640,256]{1,0:T(8,128)(2,1)}, bf16[640,256]{1,0:T(8,128)(2,1)}, u32[]{:S(2)}, u32[]{:S(2)}) collective-permute-start(bf16[640,256]{1,0:T(8,128)(2,1)} %get-tuple-element.20), channel_id=1, source_target_pairs={{0,64},{64,128},{128,192},{192,256},{256,320},{320,384},{384,448},... | collective-permute-start | bytes 983048 | tf_op jit(solution)/shard_map/ppermute | solution.py:12
  21.7 17.1 %copy-start.1 = (bf16[1,1,1280,256]{2,3,1,0:T(8,128)(2,1)S(1)}, bf16[1,1,1280,256]{2,3,1,0:T(8,128)(2,1)}, u32[]{:S(2)}) copy-start(bf16[1,1,1280,256]{2,3,1,0:T(8,128)(2,1)} %copy.3) | copy-start | bytes 1966084
  21.8 7.1 %collective-permute-start.2 = (bf16[640,256]{0,1:T(8,128)(2,1)S(1)}, bf16[640,256]{0,1:T(8,128)(2,1)S(1)}, u32[]{:S(2)}, u32[]{:S(2)}) collective-permute-start(bf16[640,256]{0,1:T(8,128)(2,1)S(1)} %get-tuple-element.17), channel_id=1, source_target_pairs={{0,1},{1,2},{2,3},{3,4},{4,5},{5,6},{6,7},{7,8},{8,9},{9,10},{10,1... | collective-permute-start | bytes 983048 | tf_op jit(solution)/shard_map/ppermute | solution.py:12
  24.9 13.9 %collective-permute-start.3 = (bf16[640,256]{0,1:T(8,128)(2,1)S(1)}, bf16[640,256]{0,1:T(8,128)(2,1)S(1)}, u32[]{:S(2)}, u32[]{:S(2)}) collective-permute-start(bf16[640,256]{0,1:T(8,128)(2,1)S(1)} %get-tuple-element.18), channel_id=1, source_target_pairs={{0,64},{64,128},{128,192},{192,256},{256,320},{320,384},{384,448},... | collective-permute-start | bytes 983048 | tf_op jit(solution)/shard_map/ppermute | solution.py:12
  40.0 6.9 %collective-permute-start.4 = (bf16[640,256]{0,1:T(8,128)(2,1)S(1)}, bf16[640,256]{0,1:T(8,128)(2,1)S(1)}, u32[]{:S(2)}, u32[]{:S(2)}) collective-permute-start(bf16[640,256]{0,1:T(8,128)(2,1)S(1)} %get-tuple-element.15), channel_id=1, source_target_pairs={{0,1},{1,2},{2,3},{3,4},{4,5},{5,6},{6,7},{7,8},{8,9},{9,10},{10,1... | collective-permute-start | bytes 983048 | tf_op jit(solution)/shard_map/ppermute | solution.py:12
  42.9 13.9 %collective-permute-start.5 = (bf16[640,256]{0,1:T(8,128)(2,1)S(1)}, bf16[640,256]{0,1:T(8,128)(2,1)S(1)}, u32[]{:S(2)}, u32[]{:S(2)}) collective-permute-start(bf16[640,256]{0,1:T(8,128)(2,1)S(1)} %get-tuple-element.16), channel_id=1, source_target_pairs={{0,64},{64,128},{128,192},{192,256},{256,320},{320,384},{384,448},... | collective-permute-start | bytes 983048 | tf_op jit(solution)/shard_map/ppermute | solution.py:12
  58.0 6.9 %collective-permute-start.6 = (bf16[640,256]{0,1:T(8,128)(2,1)S(1)}, bf16[640,256]{0,1:T(8,128)(2,1)S(1)}, u32[]{:S(2)}, u32[]{:S(2)}) collective-permute-start(bf16[640,256]{0,1:T(8,128)(2,1)S(1)} %get-tuple-element.13), channel_id=1, source_target_pairs={{0,1},{1,2},{2,3},{3,4},{4,5},{5,6},{6,7},{7,8},{8,9},{9,10},{10,1... | collective-permute-start | bytes 983048 | tf_op jit(solution)/shard_map/ppermute | solution.py:12
  60.9 13.9 %collective-permute-start.7 = (bf16[640,256]{0,1:T(8,128)(2,1)S(1)}, bf16[640,256]{0,1:T(8,128)(2,1)S(1)}, u32[]{:S(2)}, u32[]{:S(2)}) collective-permute-start(bf16[640,256]{0,1:T(8,128)(2,1)S(1)} %get-tuple-element.14), channel_id=1, source_target_pairs={{0,64},{64,128},{128,192},{192,256},{256,320},{320,384},{384,448},... | collective-permute-start | bytes 983048 | tf_op jit(solution)/shard_map/ppermute | solution.py:12
  76.0 6.9 %collective-permute-start.8 = (bf16[640,256]{0,1:T(8,128)(2,1)S(1)}, bf16[640,256]{0,1:T(8,128)(2,1)S(1)}, u32[]{:S(2)}, u32[]{:S(2)}) collective-permute-start(bf16[640,256]{0,1:T(8,128)(2,1)S(1)} %get-tuple-element.11), channel_id=1, source_target_pairs={{0,1},{1,2},{2,3},{3,4},{4,5},{5,6},{6,7},{7,8},{8,9},{9,10},{10,1... | collective-permute-start | bytes 983048 | tf_op jit(solution)/shard_map/ppermute | solution.py:12
  78.9 13.9 %collective-permute-start.9 = (bf16[640,256]{0,1:T(8,128)(2,1)S(1)}, bf16[640,256]{0,1:T(8,128)(2,1)S(1)}, u32[]{:S(2)}, u32[]{:S(2)}) collective-permute-start(bf16[640,256]{0,1:T(8,128)(2,1)S(1)} %get-tuple-element.12), channel_id=1, source_target_pairs={{0,64},{64,128},{128,192},{192,256},{256,320},{320,384},{384,448},... | collective-permute-start | bytes 983048 | tf_op jit(solution)/shard_map/ppermute | solution.py:12
  94.0 6.9 %collective-permute-start.10 = (bf16[640,256]{0,1:T(8,128)(2,1)S(1)}, bf16[640,256]{0,1:T(8,128)(2,1)S(1)}, u32[]{:S(2)}, u32[]{:S(2)}) collective-permute-start(bf16[640,256]{0,1:T(8,128)(2,1)S(1)} %get-tuple-element.9), channel_id=1, source_target_pairs={{0,1},{1,2},{2,3},{3,4},{4,5},{5,6},{6,7},{7,8},{8,9},{9,10},{10,1... | collective-permute-start | bytes 983048 | tf_op jit(solution)/shard_map/ppermute | solution.py:12
  96.9 14.0 %collective-permute-start.11 = (bf16[640,256]{0,1:T(8,128)(2,1)S(1)}, bf16[640,256]{0,1:T(8,128)(2,1)S(1)}, u32[]{:S(2)}, u32[]{:S(2)}) collective-permute-start(bf16[640,256]{0,1:T(8,128)(2,1)S(1)} %get-tuple-element.10), channel_id=1, source_target_pairs={{0,64},{64,128},{128,192},{192,256},{256,320},{320,384},{384,448},... | collective-permute-start | bytes 983048 | tf_op jit(solution)/shard_map/ppermute | solution.py:12
  112.0 6.7 %collective-permute-start.12 = (bf16[640,256]{0,1:T(8,128)(2,1)S(1)}, bf16[640,256]{0,1:T(8,128)(2,1)S(1)}, u32[]{:S(2)}, u32[]{:S(2)}) collective-permute-start(bf16[640,256]{0,1:T(8,128)(2,1)S(1)} %get-tuple-element.7), channel_id=1, source_target_pairs={{0,1},{1,2},{2,3},{3,4},{4,5},{5,6},{6,7},{7,8},{8,9},{9,10},{10,1... | collective-permute-start | bytes 983048 | tf_op jit(solution)/shard_map/ppermute | solution.py:12
  114.8 13.9 %collective-permute-start.13 = (bf16[640,256]{0,1:T(8,128)(2,1)S(1)}, bf16[640,256]{0,1:T(8,128)(2,1)S(1)}, u32[]{:S(2)}, u32[]{:S(2)}) collective-permute-start(bf16[640,256]{0,1:T(8,128)(2,1)S(1)} %get-tuple-element.8), channel_id=1, source_target_pairs={{0,64},{64,128},{128,192},{192,256},{256,320},{320,384},{384,448},... | collective-permute-start | bytes 983048 | tf_op jit(solution)/shard_map/ppermute | solution.py:12
  129.8 6.8 %collective-permute-start.14 = (bf16[640,256]{0,1:T(8,128)(2,1)S(1)}, bf16[640,256]{0,1:T(8,128)(2,1)S(1)}, u32[]{:S(2)}, u32[]{:S(2)}) collective-permute-start(bf16[640,256]{0,1:T(8,128)(2,1)S(1)} %get-tuple-element.5), channel_id=1, source_target_pairs={{0,1},{1,2},{2,3},{3,4},{4,5},{5,6},{6,7},{7,8},{8,9},{9,10},{10,1... | collective-permute-start | bytes 983048 | tf_op jit(solution)/shard_map/ppermute | solution.py:12
  132.6 13.9 %collective-permute-start.15 = (bf16[640,256]{0,1:T(8,128)(2,1)S(1)}, bf16[640,256]{0,1:T(8,128)(2,1)S(1)}, u32[]{:S(2)}, u32[]{:S(2)}) collective-permute-start(bf16[640,256]{0,1:T(8,128)(2,1)S(1)} %get-tuple-element.6), channel_id=1, source_target_pairs={{0,64},{64,128},{128,192},{192,256},{256,320},{320,384},{384,448},... | collective-permute-start | bytes 983048 | tf_op jit(solution)/shard_map/ppermute | solution.py:12
where the time goes:
time: 151 us
  waiting for transfers between devices  90.5 us (60%)
  starting transfers between devices  42.1 us (28%)
  matrix products  10.8 us (7%)
  local copies, waits for them, and re-layouts  6.87 us (5%)
    ppermute x16, waiting for transfers between devices, shifted(): return lax.ppermute(array, axis, pairs)  90.5 us
    ppermute x16, starting transfers between devices, shifted(): return lax.ppermute(array, axis, pairs)  42.1 us
    dot_general x8, matrix products, update(): jnp.dot(mapping, incoming, preferred_element_type=jnp.float32)  10.8 us
  transfers between devices with their start and end apart: 16, of which 15 were waited for; matrix products, arithmetic and copies ran while one was open for 1% of the time, Pallas kernels for 0%

commit v1 on v0

v1 whole, which is shorter than its diff:
```python
import functools

import jax
import jax.numpy as jnp
from jax import lax
from jax.experimental import pallas as pl
from jax.experimental.pallas import tpu as pltpu
from jax.sharding import PartitionSpec as P

ITERS = 8
PARTS = 2
MESH = pl.DeviceIdType.MESH


def kernel(rows, cols, maps, sources, traces, mapping, state, left, below, total,
           load_sem, map_sem, right_sent, up_sent, left_got, below_got):
    half = left.shape[2]
    width = left.shape[3]
    row, col = lax.axis_index("row"), lax.axis_index("col")
    has_left, has_below = col > 0, row > 0
    has_right, has_above = col < cols - 1, row < rows - 1

    def lanes(part):
        return pl.ds(part * width, width)

    loads = [pltpu.make_async_copy(sources.at[0, 0, :, lanes(part)], state.at[0, part], load_sem.at[part])
             for part in range(PARTS)]
    for load in loads:
        load.start()
    map_load = pltpu.make_async_copy(maps.at[0, 0], mapping, map_sem)
    map_load.start()

    barrier = pltpu.get_barrier_semaphore()

    @pl.when(has_left)
    def _():
        pl.semaphore_signal(barrier, inc=1, device_id={"col": col - 1}, device_id_type=MESH)

    @pl.when(has_below)
    def _():
        pl.semaphore_signal(barrier, inc=1, device_id={"row": row - 1}, device_id_type=MESH)

    @pl.when(has_right | has_above)
    def _():
        pl.semaphore_wait(barrier, has_right.astype(jnp.int32) + has_above.astype(jnp.int32))

    def to_right(step, part):
        return pltpu.make_async_remote_copy(
            src_ref=state.at[step, part, pl.ds(0, half)], dst_ref=left.at[step, part],
            send_sem=right_sent.at[step, part], recv_sem=left_got.at[step, part],
            device_id={"col": lax.rem(col + 1, cols)}, device_id_type=MESH)

    def to_above(step, part):
        return pltpu.make_async_remote_copy(
            src_ref=state.at[step, part, pl.ds(half, half)], dst_ref=below.at[step, part],
            send_sem=up_sent.at[step, part], recv_sem=below_got.at[step, part],
            device_id={"row": lax.rem(row + 1, rows)}, device_id_type=MESH)

    for part in range(PARTS):
        loads[part].wait()

        @pl.when(has_above)
        def _():
            to_above(0, part).start()

        @pl.when(has_right)
        def _():
            to_right(0, part).start()

    @pl.when(jnp.logical_not(has_left))
    def _():
        left[ITERS] = jnp.zeros_like(left[ITERS])

    @pl.when(jnp.logical_not(has_below))
    def _():
        below[ITERS] = jnp.zeros_like(below[ITERS])

    map_load.wait()

    def advance(step, part, last):
        @pl.when(has_left)
        def _():
            to_right(step, part).wait_recv()

        total[...] = state[0, part].astype(jnp.float32) + jnp.dot(
            mapping[:, :half], left[jnp.where(has_left, step, ITERS), part],
            preferred_element_type=jnp.float32)

        @pl.when(has_below)
        def _():
            to_above(step, part).wait_recv()

        arrived = below[jnp.where(has_below, step, ITERS), part]
        upper = (total[half:] + jnp.dot(
            mapping[half:, half:], arrived, preferred_element_type=jnp.float32)).astype(jnp.bfloat16)
        if last:
            traces[0, 0, half:, part * width:(part + 1) * width] = upper
        else:
            state[step + 1, part, half:] = upper

            @pl.when(has_above)
            def _():
                to_above(step + 1, part).start()

        right = (total[:half] + jnp.dot(
            mapping[:half, half:], arrived, preferred_element_type=jnp.float32)).astype(jnp.bfloat16)
        if last:
            traces[0, 0, :half, part * width:(part + 1) * width] = right
        else:
            state[step + 1, part, :half] = right

            @pl.when(has_right)
            def _():
                to_right(step + 1, part).start()

    def one_step(step, carry):
        for part in range(PARTS):
            advance(step, part, False)
        return carry

    lax.fori_loop(0, ITERS - 1, one_step, 0)
    for part in range(PARTS):
        advance(ITERS - 1, part, True)

    def drain(step, carry):
        for part in range(PARTS):
            @pl.when(has_above)
            def _():
                to_above(step, part).wait_send()

            @pl.when(has_right)
            def _():
                to_right(step, part).wait_send()
        return carry

    lax.fori_loop(0, ITERS, drain, 0)


def per_device(rows, cols, trace_maps, sources):
    order, count = sources.shape[2:]
    half, width = order // 2, count // PARTS
    bf16, dma = jnp.bfloat16, pltpu.SemaphoreType.DMA
    return pl.pallas_call(
        functools.partial(kernel, rows, cols),
        out_shape=jax.ShapeDtypeStruct(sources.shape, bf16),
        in_specs=[pl.BlockSpec(memory_space=pltpu.HBM)] * 2,
        out_specs=pl.BlockSpec(memory_space=pltpu.VMEM),
        scratch_shapes=[
            pltpu.VMEM((order, order), bf16),
            pltpu.VMEM((ITERS, PARTS, order, width), bf16),
            pltpu.VMEM((ITERS + 1, PARTS, half, width), bf16),
            pltpu.VMEM((ITERS + 1, PARTS, half, width), bf16),
            pltpu.VMEM((order, width), jnp.float32),
            dma((PARTS,)),
            dma,
            dma((ITERS, PARTS)),
            dma((ITERS, PARTS)),
            dma((ITERS, PARTS)),
            dma((ITERS, PARTS)),
        ],
        compiler_params=pltpu.CompilerParams(
            collective_id=0, has_side_effects=True, vmem_limit_bytes=60 << 20),
    )(trace_maps, sources)


def solution(mesh):
    placed = P("row", "col", None, None)
    return jax.shard_map(
        functools.partial(per_device, mesh.shape["row"], mesh.shape["col"]),
        mesh=mesh,
        in_specs=(placed, placed),
        out_specs=placed,
        check_vma=False,
    )
```

time: 151 us -> 103 us (0.68)
  the two profiles are of different devices: /device:TPU:271 before, /device:TPU:4 now
where the time goes in v1:
time: 103 us
  Pallas kernels  101 us (98%)
  local copies, waits for them, and re-layouts  1.97 us (2%)
    pallas_call x1, Pallas kernels, per_device(): pl.pallas_call(functools.partial(kernel, rows, cols), out_shape=jax.Shape...  101 us

profile of v1, /device:TPU:4, one launch (start us, length us, event | category | flops | bytes accessed | tf_op | source)
XLA Modules:
  0.0 102.7 jit_solution(9154632031598220042)
XLA Ops:
  0.0 100.7 %shard_map.28 = bf16[1,1,1280,256]{3,2,1,0:T(8,128)(2,1)} custom-call(bf16[1,1,1280,1280]{3,2,1,0:T(8,128)(2,1)} %maps.1, bf16[1,1,1280,256]{3,2,1,0:T(8,128)(2,1)} %sources.1), custom_call_target="tpu_custom_call" | custom-call | tf_op jit(solution)/shard_map/pallas_call | solution.py:143
  100.7 2.0 %copy.4 = bf16[1,1,1280,256]{3,2,1,0:T(8,128)(2,1)} copy(bf16[1,1,1280,256]{3,2,1,0:T(8,128)(2,1)} %shard_map.28) | data formatting | bytes 1310720

commit v2 on v1

--- a/solution.py
+++ b/solution.py
@@ -8,17 +8,23 @@
 from jax.sharding import PartitionSpec as P
 
 ITERS = 8
+RUN = 32
+PIECES = ((0, 2, 112, 0, 1), (13, 15, 112, 224, 0), (2, 3, 96, 448, 1), (12, 13, 96, 544, 0))
 PARTS = 2
 MESH = pl.DeviceIdType.MESH
 
 
-def kernel(rows, cols, maps, sources, traces, mapping, state, left, below, total,
-           load_sem, map_sem, right_sent, up_sent, left_got, below_got):
+def kernel(rows, cols, maps, sources, traces, mapping, state, left, below, seam, total,
+           load_sem, map_sem, right_sent, up_sent, left_got, below_got, seam_sent, seam_got):
     half = left.shape[2]
     width = left.shape[3]
     row, col = lax.axis_index("row"), lax.axis_index("col")
     has_left, has_below = col > 0, row > 0
     has_right, has_above = col < cols - 1, row < rows - 1
+    before_seam, after_seam = col == RUN - 1, col == RUN
+    chip = (col - RUN) // 2
+    passes = [(col % 2 == core) & (chip >= max(first, 1)) & (chip < end) for first, end, _, _, core in PIECES]
+    on_seam = functools.reduce(jnp.logical_or, passes)
 
     def lanes(part):
         return pl.ds(part * width, width)
@@ -40,9 +46,20 @@
     def _():
         pl.semaphore_signal(barrier, inc=1, device_id={"row": row - 1}, device_id_type=MESH)
 
-    @pl.when(has_right | has_above)
-    def _():
-        pl.semaphore_wait(barrier, has_right.astype(jnp.int32) + has_above.astype(jnp.int32))
+    @pl.when(on_seam)
+    def _():
+        pl.semaphore_signal(barrier, inc=1, device_id={"col": RUN - 1}, device_id_type=MESH)
+
+    @pl.when(after_seam)
+    def _():
+        for first, end, _, _, core in PIECES:
+            for other in range(max(first, 1), end):
+                pl.semaphore_signal(barrier, inc=1, device_id={"col": RUN + core + 2 * other}, device_id_type=MESH)
+
+    @pl.when(has_right | has_above | on_seam)
+    def _():
+        pl.semaphore_wait(barrier, has_right.astype(jnp.int32) + has_above.astype(jnp.int32)
+                          + on_seam.astype(jnp.int32) + (sum(end - first for first, end, *_ in PIECES) - 1) * before_seam.astype(jnp.int32))
 
     def to_right(step, part):
         return pltpu.make_async_remote_copy(
@@ -56,6 +73,53 @@
             send_sem=up_sent.at[step, part], recv_sem=below_got.at[step, part],
             device_id={"row": lax.rem(row + 1, rows)}, device_id_type=MESH)
 
+    def straight(step, part):
+        tall = PIECES[0][2]
+        return pltpu.make_async_remote_copy(
+            src_ref=state.at[step, part, pl.ds(0, tall)], dst_ref=left.at[step, part, pl.ds(0, tall)],
+            send_sem=right_sent.at[step, part], recv_sem=left_got.at[step, part],
+            device_id={"col": RUN}, device_id_type=MESH)
+
+    def rows_of(kind, other):
+        first, _, tall, start, _ = PIECES[kind]
+        return pl.ds(pl.multiple_of(start + (other - first) * tall, 8), tall)
+
+    def to_seam(step, part, kind, other):
+        return pltpu.make_async_remote_copy(
+            src_ref=state.at[step, part, rows_of(kind, other)],
+            dst_ref=seam.at[step, part, pl.ds(0, PIECES[kind][2])],
+            send_sem=right_sent.at[step, part], recv_sem=seam_got.at[step, part],
+            device_id={"col": RUN + PIECES[kind][4] + 2 * other}, device_id_type=MESH)
+
+    def from_seam(step, part, kind):
+        return pltpu.make_async_remote_copy(
+            src_ref=seam.at[step, part, pl.ds(0, PIECES[kind][2])],
+            dst_ref=left.at[step, part, rows_of(kind, chip)],
+            send_sem=seam_sent.at[step, part], recv_sem=left_got.at[step, part],
+            device_id={"col": RUN}, device_id_type=MESH)
+
+    def send_right(step, part):
+        @pl.when(has_right & jnp.logical_not(before_seam))
+        def _():
+            to_right(step, part).start()
+
+        @pl.when(before_seam)
+        def _():
+            for kind in reversed(range(len(PIECES))):
+                def send(other, carry):
+                    to_seam(step, part, kind, other).start()
+                    return carry
+
+                lax.fori_loop(max(PIECES[kind][0], 1), PIECES[kind][1], send, 0)
+            straight(step, part).start()
+
+    def pass_on(step, part):
+        for kind in range(len(PIECES)):
+            @pl.when(passes[kind])
+            def _():
+                to_seam(step, part, kind, chip).wait_recv()
+                from_seam(step, part, kind).start()
+
     for part in range(PARTS):
         loads[part].wait()
 
@@ -63,9 +127,7 @@
         def _():
             to_above(0, part).start()
 
-        @pl.when(has_right)
-        def _():
-            to_right(0, part).start()
+        send_right(0, part)
 
     @pl.when(jnp.logical_not(has_left))
     def _():
@@ -76,6 +138,9 @@
         below[ITERS] = jnp.zeros_like(below[ITERS])
 
     map_load.wait()
+
+    for part in range(PARTS):
+        pass_on(0, part)
 
     def advance(step, part, last):
         @pl.when(has_left)
@@ -102,6 +167,11 @@
             def _():
                 to_above(step + 1, part).start()
 
+        if part == PARTS - 1 and not last:
+            pass_on(step + 1, 0)
+        elif part < PARTS - 1:
+            pl.when(step > 0)(lambda: pass_on(step, part + 1))
+
         right = (total[:half] + jnp.dot(
             mapping[:half, half:], arrived, preferred_element_type=jnp.float32)).astype(jnp.bfloat16)
         if last:
@@ -109,9 +179,7 @@
         else:
             state[step + 1, part, :half] = right
 
-            @pl.when(has_right)
-            def _():
-                to_right(step + 1, part).start()
+            send_right(step + 1, part)
 
     def one_step(step, carry):
         for part in range(PARTS):
@@ -131,6 +199,11 @@
             @pl.when(has_right)
             def _():
                 to_right(step, part).wait_send()
+
+            for kind in range(len(PIECES)):
+                @pl.when(passes[kind])
+                def _():
+                    from_seam(step, part, kind).wait_send()
         return carry
 
     lax.fori_loop(0, ITERS, drain, 0)
@@ -150,6 +223,7 @@
             pltpu.VMEM((ITERS, PARTS, order, width), bf16),
             pltpu.VMEM((ITERS + 1, PARTS, half, width), bf16),
             pltpu.VMEM((ITERS + 1, PARTS, half, width), bf16),
+            pltpu.VMEM((ITERS, PARTS, max(piece[2] for piece in PIECES), width), bf16),
             pltpu.VMEM((order, width), jnp.float32),
             dma((PARTS,)),
             dma,
@@ -157,10 +231,12 @@
             dma((ITERS, PARTS)),
             dma((ITERS, PARTS)),
             dma((ITERS, PARTS)),
+            dma((ITERS, PARTS)),
+            dma((ITERS, PARTS)),
         ],
         compiler_params=pltpu.CompilerParams(
-            collective_id=0, has_side_effects=True, vmem_limit_bytes=60 << 20),
-    )(trace_maps, sources)
+            collective_id=0, has_side_effects=True, vmem_limit_bytes=48 << 20),
+    )(*(pltpu.with_memory_space_constraint(array, pltpu.HBM) for array in (trace_maps, sources)))
 
 
 def solution(mesh):

time: 103 us -> 76.7 us (0.74)
  the two profiles are of different devices: /device:TPU:4 before, /device:TPU:14 now
where the time goes in v2:
time: 76.7 us; the launch traced here: 76.6 us
  Pallas kernels  75.7 us (99%)
  local copies, waits for them, and re-layouts  0.84 us (1%)
    pallas_call x1, Pallas kernels, per_device(): pl.pallas_call(functools.partial(kernel, rows, cols), out_shape=jax.Shape...  75.7 us

profile of v2, /device:TPU:14, one launch (start us, length us, event | category | flops | bytes accessed | tf_op | source)
XLA Modules:
  0.0 76.6 jit_solution(9959611410346512304)
XLA Ops:
  0.0 75.7 %shard_map.28 = bf16[1,1,1280,256]{3,2,1,0:T(8,128)(2,1)S(1)} custom-call(bf16[1,1,1280,1280]{3,2,1,0:T(8,128)(2,1)} %maps.1, bf16[1,1,1280,256]{3,2,1,0:T(8,128)(2,1)} %sources.1), custom_call_target="tpu_custom_call" | custom-call | tf_op jit(solution)/shard_map/pallas_call | solution.py:216
  75.7 0.8 %copy.4 = bf16[1,1,1280,256]{3,2,1,0:T(8,128)(2,1)} copy(bf16[1,1,1280,256]{3,2,1,0:T(8,128)(2,1)S(1)} %shard_map.28) | data formatting | bytes 1310720

commit v3 on v2

--- a/solution.py
+++ b/solution.py
@@ -9,7 +9,7 @@
 
 ITERS = 8
 RUN = 32
-PIECES = ((0, 2, 112, 0, 1), (13, 15, 112, 224, 0), (2, 3, 96, 448, 1), (12, 13, 96, 544, 0))
+PIECES = ((0, 1, 96, 0, 1), (1, 3, 184, 96, 1), (3, 4, 176, 464, 1))
 PARTS = 2
 MESH = pl.DeviceIdType.MESH
 
@@ -127,7 +127,9 @@
         def _():
             to_above(0, part).start()
 
-        send_right(0, part)
+        @pl.when(has_right)
+        def _():
+            to_right(0, part).start()
 
     @pl.when(jnp.logical_not(has_left))
     def _():
@@ -138,9 +140,6 @@
         below[ITERS] = jnp.zeros_like(below[ITERS])
 
     map_load.wait()
-
-    for part in range(PARTS):
-        pass_on(0, part)
 
     def advance(step, part, last):
         @pl.when(has_left)
@@ -150,6 +149,11 @@
         total[...] = state[0, part].astype(jnp.float32) + jnp.dot(
             mapping[:, :half], left[jnp.where(has_left, step, ITERS), part],
             preferred_element_type=jnp.float32)
+
+        if part == PARTS - 1 and not last:
+            pass_on(step + 1, 0)
+        elif part < PARTS - 1:
+            pl.when(step > 0)(lambda: pass_on(step, part + 1))
 
         @pl.when(has_below)
         def _():
@@ -167,11 +171,6 @@
             def _():
                 to_above(step + 1, part).start()
 
-        if part == PARTS - 1 and not last:
-            pass_on(step + 1, 0)
-        elif part < PARTS - 1:
-            pl.when(step > 0)(lambda: pass_on(step, part + 1))
-
         right = (total[:half] + jnp.dot(
             mapping[:half, half:], arrived, preferred_element_type=jnp.float32)).astype(jnp.bfloat16)
         if last:
@@ -201,7 +200,7 @@
                 to_right(step, part).wait_send()
 
             for kind in range(len(PIECES)):
-                @pl.when(passes[kind])
+                @pl.when(passes[kind] & (step > 0))
                 def _():
                     from_seam(step, part, kind).wait_send()
         return carry

time: 76.7 us -> 73.8 us (0.962)
  the two profiles are of different devices: /device:TPU:14 before, /device:TPU:2 now
where the time goes in v3:
time: 73.8 us; the launch traced here: 73.7 us
  Pallas kernels  72.9 us (99%)
  local copies, waits for them, and re-layouts  0.84 us (1%)
    pallas_call x1, Pallas kernels, per_device(): pl.pallas_call(functools.partial(kernel, rows, cols), out_shape=jax.Shape...  72.9 us

profile of v3, /device:TPU:2, one launch (start us, length us, event | category | flops | bytes accessed | tf_op | source)
XLA Modules:
  0.0 73.7 jit_solution(8985341051538821388)
XLA Ops:
  0.0 72.9 %shard_map.28 = bf16[1,1,1280,256]{3,2,1,0:T(8,128)(2,1)S(1)} custom-call(bf16[1,1,1280,1280]{3,2,1,0:T(8,128)(2,1)} %maps.1, bf16[1,1,1280,256]{3,2,1,0:T(8,128)(2,1)} %sources.1), custom_call_target="tpu_custom_call" | custom-call | tf_op jit(solution)/shard_map/pallas_call | solution.py:215
  72.9 0.8 %copy.4 = bf16[1,1,1280,256]{3,2,1,0:T(8,128)(2,1)} copy(bf16[1,1,1280,256]{3,2,1,0:T(8,128)(2,1)S(1)} %shard_map.28) | data formatting | bytes 1310720

commit v4 on v3

--- a/solution.py
+++ b/solution.py
@@ -29,32 +29,30 @@
     def lanes(part):
         return pl.ds(part * width, width)
 
+    barrier = pltpu.get_barrier_semaphore()
+
+    @pl.when(has_left)
+    def _():
+        pl.semaphore_signal(barrier, inc=1, device_id={"col": col - 1}, device_id_type=MESH)
+
+    @pl.when(has_below)
+    def _():
+        pl.semaphore_signal(barrier, inc=1, device_id={"row": row - 1}, device_id_type=MESH)
+
+    @pl.when(on_seam)
+    def _():
+        pl.semaphore_signal(barrier, inc=1, device_id={"col": RUN - 1}, device_id_type=MESH)
+
+    @pl.when(after_seam)
+    def _():
+        for first, end, _, _, core in PIECES:
+            for other in range(max(first, 1), end):
+                pl.semaphore_signal(barrier, inc=1, device_id={"col": RUN + core + 2 * other}, device_id_type=MESH)
+
     loads = [pltpu.make_async_copy(sources.at[0, 0, :, lanes(part)], state.at[0, part], load_sem.at[part])
              for part in range(PARTS)]
     for load in loads:
         load.start()
-    map_load = pltpu.make_async_copy(maps.at[0, 0], mapping, map_sem)
-    map_load.start()
-
-    barrier = pltpu.get_barrier_semaphore()
-
-    @pl.when(has_left)
-    def _():
-        pl.semaphore_signal(barrier, inc=1, device_id={"col": col - 1}, device_id_type=MESH)
-
-    @pl.when(has_below)
-    def _():
-        pl.semaphore_signal(barrier, inc=1, device_id={"row": row - 1}, device_id_type=MESH)
-
-    @pl.when(on_seam)
-    def _():
-        pl.semaphore_signal(barrier, inc=1, device_id={"col": RUN - 1}, device_id_type=MESH)
-
-    @pl.when(after_seam)
-    def _():
-        for first, end, _, _, core in PIECES:
-            for other in range(max(first, 1), end):
-                pl.semaphore_signal(barrier, inc=1, device_id={"col": RUN + core + 2 * other}, device_id_type=MESH)
 
     @pl.when(has_right | has_above | on_seam)
     def _():
@@ -130,6 +128,9 @@
         @pl.when(has_right)
         def _():
             to_right(0, part).start()
+
+    map_load = pltpu.make_async_copy(maps.at[0, 0], mapping, map_sem)
+    map_load.start()
 
     @pl.when(jnp.logical_not(has_left))
     def _():

time: 73.8 us -> 73.9 us (level)
  no operation moved by 1% of the time
where the time goes in v4:
time: 73.9 us; the launch traced here: 73.7 us
  Pallas kernels  72.9 us (99%)
  local copies, waits for them, and re-layouts  0.84 us (1%)
    pallas_call x1, Pallas kernels, per_device(): pl.pallas_call(functools.partial(kernel, rows, cols), out_shape=jax.Shape...  72.9 us

profile of v4, /device:TPU:2, one launch (start us, length us, event | category | flops | bytes accessed | tf_op | source)
XLA Modules:
  0.0 73.7 jit_solution(13951360269608219315)
XLA Ops:
  0.0 72.9 %shard_map.28 = bf16[1,1,1280,256]{3,2,1,0:T(8,128)(2,1)S(1)} custom-call(bf16[1,1,1280,1280]{3,2,1,0:T(8,128)(2,1)} %maps.1, bf16[1,1,1280,256]{3,2,1,0:T(8,128)(2,1)} %sources.1), custom_call_target="tpu_custom_call" | custom-call | tf_op jit(solution)/shard_map/pallas_call | solution.py:216
  72.9 0.8 %copy.4 = bf16[1,1,1280,256]{3,2,1,0:T(8,128)(2,1)} copy(bf16[1,1,1280,256]{3,2,1,0:T(8,128)(2,1)S(1)} %shard_map.28) | data formatting | bytes 1310720
